TPU v7x, 32 devices: a whole 2x2x4 slice. The times are simulated.
32 devices in a mesh: cell: 16 (over z, x, core), gene: 2 (over y).
Axes of the slice: x: 2, y: 2, z: 4, core: 2. Of those that a mesh axis runs over, the one named last changes fastest.
Arguments:
- counts: bfloat16 [15360, 16384], P('cell', 'gene'), as said below
- w_factor: float32 [15360, 128], P('cell'), may hold values from 0.004 to 2, as said below
- h_factor: float32 [128, 16384], P('cell', 'gene'), may hold values from 0.03 to 0.3, as said below
Outputs:
- w_updated: float32 [15360, 128], P('cell')
- h_updated: float32 [128, 16384], P('cell', 'gene')
Inputs may be any that keep to these rules, and one draw needn't show every extreme that they name: `counts`: nonnegative whole numbers. `w_factor`: positive. `h_factor`: positive.
All inputs are finite; a program needn't handle non-finite values.
Results may differ from a plain program's by a relative error of at most 0.00092.
Values may be sent and summed in bfloat16 or wider, within the bound.
No kernel may reach another device: no remote copies, remote signals or barrier semaphores. Data moves between devices by JAX's collectives and lax.ppermute only.
A program may use at most 64 MiB of HBM per device.

v0:
```python
import jax
import jax.numpy as jnp
from jax import lax
from jax.sharding import PartitionSpec as P


def per_device(counts, w_factor, h_factor):
    own_rows = h_factor.shape[0]
    rank = w_factor.shape[1]
    w_copy = w_factor.astype(jnp.bfloat16)
    row_offset = lax.axis_index("cell") * own_rows
    counts_float = counts.astype(jnp.float32)
    columns = w_copy
    modeled = jnp.dot(
        columns,
        lax.all_gather(h_factor.astype(jnp.bfloat16), "cell", axis=0, tiled=True),
        preferred_element_type=jnp.float32,
    )
    quotient = (counts_float / modeled).astype(jnp.bfloat16)
    columns = w_copy
    numerator = lax.psum_scatter(
        lax.dot_general(
            columns, quotient, (((0,), (0,)), ((), ())), preferred_element_type=jnp.float32
        ),
        "cell",
        scatter_dimension=0,
        tiled=True,
    )
    w_totals = lax.psum(jnp.sum(w_factor, axis=0), "cell")
    own_totals = lax.dynamic_slice_in_dim(w_totals, row_offset, own_rows, 0)
    h_updated = h_factor * numerator / own_totals[:, None]
    h_new_copy = lax.all_gather(h_updated.astype(jnp.bfloat16), "cell", axis=0, tiled=True)
    modeled_again = jnp.dot(w_copy, h_new_copy, preferred_element_type=jnp.float32)
    quotient_again = (counts_float / modeled_again).astype(jnp.bfloat16)
    partial_w = lax.dot_general(
        quotient_again, h_new_copy, (((1,), (1,)), ((), ())), preferred_element_type=jnp.float32
    )
    partial_totals = jnp.sum(h_new_copy.astype(jnp.float32), axis=1)
    w_share = lax.psum_scatter(partial_w, "gene", scatter_dimension=1, tiled=True)
    h_totals = lax.psum(partial_totals, "gene")
    share_width = rank // lax.axis_size("gene")
    col_offset = lax.axis_index("gene") * share_width
    w_own = lax.dynamic_slice_in_dim(w_factor, col_offset, share_width, 1)
    totals_own = lax.dynamic_slice_in_dim(h_totals, col_offset, share_width, 0)
    w_part = w_own * w_share / totals_own[None, :]
    w_updated = lax.all_gather(w_part, "gene", axis=1, tiled=True)
    return (w_updated, h_updated)


def solution(mesh):
    in_specs = (P("cell", "gene"), P("cell", None), P("cell", "gene"))
    out_specs = (P("cell", None), P("cell", "gene"))
    return jax.shard_map(
        per_device, mesh=mesh, in_specs=in_specs, out_specs=out_specs, check_vma=False
    )
```

profile of v0, /device:TPU:0, one launch (start us, length us, event | category | flops | bytes accessed | tf_op | source)
XLA Modules:
  0.0 248.2 jit_solution(8995357598601707280)
XLA Ops:
  7.2 0.0 all-gather.3.cloned.1.call-start
  7.2 1.6 convert_element_type.23
  8.8 0.0 all-gather.3.cloned.1.call-update
  8.9 0.0 reduce-scatter.7.cloned.1.call-start
  8.9 46.0 %all-gather.3.cloned.1.call-done = bf16[128,8192]{1,0:T(8,128)(2,1)} async-done(((bf16[8,8192]{1,0:T(8,128)(2,1)}), bf16[128,8192]{1,0:T(8,128)(2,1)}) %all-gather.3.cloned.1.call-update) | async-done | bytes 2097168 | tf_op jit(solution)/shard_map/all_gather | solution.py:16
  54.9 16.7 %fusion.4 = f32[128,8192]{0,1:T(8,128)} fusion(bf16[960,8192]{1,0:T(8,128)(2,1)} %param.3, bf16[128,8192]{1,0:T(8,128)(2,1)} %all-gather.3.cloned.1.call-done, f32[960,128]{1,0:T(8,128)} %param.4), kind=kOutput, calls=%fused_computation.5 | convolution fusion | flops 4050370560 | bytes 22511616 | tf_op jit(solution)/shard_map/dot_general | solution.py:22
  71.6 5.6 %copy.14 = f32[128,8192]{1,0:T(8,128)} copy(f32[128,8192]{0,1:T(8,128)} %fusion.4) | data formatting | bytes 8388608
  77.3 0.0 reduce-scatter.7.cloned.1.call-update
  77.3 0.0 all-gather.5.cloned.1.call-start
  77.3 0.9 copy-done.2
  78.2 2.6 %copy.10 = f32[8,8192]{0,1:T(8,128)} copy(f32[8,8192]{1,0:T(8,128)S(1)} %copy-done.2) | data formatting | bytes 524288 | tf_op args[2]
  80.8 0.1 reduce_sum.18
  80.9 31.7 %psum.14 = f32[128]{0:T(128)S(1)} all-reduce(f32[128]{0:T(128)S(1)} %reduce_sum.18), channel_id=1, replica_groups=mesh['cell'=16,'gene'=2] {'cell'}, use_global_device_ids=true, to_apply=%region_2.0 | all-reduce | flops 128 | bytes 1024 | tf_op jit(solution)/shard_map/psum | solution.py:29
  112.6 0.1 dynamic_slice.10
  112.7 36.1 %reduce-scatter.7.cloned.1.call-done = f32[8,8192]{1,0:T(8,128)} async-done(((f32[128,8192]{1,0:T(8,128)}), f32[8,8192]{1,0:T(8,128)}) %reduce-scatter.7.cloned.1.call-update) | async-done | bytes 262160
  148.7 3.5 %copy.15 = f32[8,8192]{0,1:T(8,128)} copy(f32[8,8192]{1,0:T(8,128)} %reduce-scatter.7.cloned.1.call-done) | data formatting | bytes 524288
  152.2 5.9 %fusion.14 = (bf16[8,8192]{0,1:T(8,128)(2,1)S(1)}, f32[8,8192]{0,1:T(8,128)}) fusion(f32[8]{0:T(128)S(1)} %dynamic_slice.10, f32[8,8192]{0,1:T(8,128)} %copy.10, f32[8,8192]{0,1:T(8,128)} %copy.15), kind=kLoop, calls=%fused_computation.14 | loop fusion | flops 196608 | bytes 917536 | tf_op jit(solution)/shard_map/convert_element_type | solution.py:32
  158.1 1.4 copy.11
  159.6 0.2 reduce-scatter.5.cloned.1.call-start
  159.8 40.4 %all-gather.5.cloned.1.call-done = bf16[128,8192]{1,0:T(8,128)(2,1)} async-done(((bf16[8,8192]{1,0:T(8,128)(2,1)}), bf16[128,8192]{1,0:T(8,128)(2,1)}) %all-gather.5.cloned.1.call-update) | async-done | bytes 2097168 | tf_op jit(solution)/shard_map/all_gather | solution.py:32
  200.2 17.3 %fusion.9 = f32[960,128]{0,1:T(8,128)} fusion(bf16[128,8192]{1,0:T(8,128)(2,1)} %all-gather.5.cloned.1.call-done, bf16[960,8192]{1,0:T(8,128)(2,1)} %param.3, f32[960,128]{1,0:T(8,128)S(1)} %copy-done.1), kind=kOutput, calls=%fused_computation.7 | convolution fusion | flops 4050247680 | bytes 18808832 | tf_op jit(solution)/shard_map/dot_general | solution.py:35
  217.5 0.0 reduce-scatter.5.cloned.1.call-update
  217.5 0.2 constant_dynamic-slice_fusion
  217.7 0.2 copy.16
  217.9 3.7 %copy.13 = f32[8,8192]{1,0:T(8,128)} copy(f32[8,8192]{0,1:T(8,128)} %get-tuple-element.7) | data formatting | bytes 524288
  221.6 0.4 convert_reduce_fusion
  221.9 5.1 %psum.15 = f32[128]{0:T(128)S(1)} all-reduce(f32[128]{0:T(128)S(1)} %convert_reduce_fusion), channel_id=1, replica_groups=mesh['cell'=16,'gene'=2] {'gene'}, use_global_device_ids=true, to_apply=%region_5.0 | all-reduce | flops 128 | bytes 1024 | tf_op jit(solution)/shard_map/psum | solution.py:40
  227.1 0.1 dynamic_slice.11
  227.1 4.0 %reduce-scatter.5.cloned.1.call-done = f32[960,64]{0,1:T(8,128)} async-done(((f32[960,128]{0,1:T(8,128)}), f32[960,64]{0,1:T(8,128)}) %reduce-scatter.5.cloned.1.call-update) | async-done | bytes 245776 | tf_op jit(solution)/shard_map/reduce_scatter | solution.py:39
  231.1 1.0 multiply_divide_fusion.1
  232.1 8.5 %all_gather.11 = f32[960,128]{0,1:T(8,128)S(1)} all-gather(f32[960,64]{0,1:T(8,128)S(1)} %multiply_divide_fusion.1), channel_id=1, replica_groups=mesh['cell'=16,'gene'=2] {'gene'}, dimensions={1}, use_global_device_ids=true | all-gather | bytes 737280 | tf_op jit(solution)/shard_map/all_gather | solution.py:46
  240.7 1.0 copy.12
  (6 shorter events, 0.0 us)
Async XLA Ops:
  7.2 47.8 %all-gather.3.cloned.1.call-start = ((), (), s32[]{:S(2)}) async-start(), calls=%async_computation.2 | async-start | bytes 2228224 | tf_op jit(solution)/shard_map/all_gather | solution.py:16
  8.9 139.9 %reduce-scatter.7.cloned.1.call-start = ((), (), s32[]{:S(2)}) async-start(), calls=%async_computation.5 | async-start | bytes 4456448
  77.2 0.9 copy-start.2
  77.3 3.5 %copy-start.1 = (f32[960,128]{1,0:T(8,128)S(1)}, f32[960,128]{1,0:T(8,128)}, u32[]{:S(2)}) copy-start(f32[960,128]{1,0:T(8,128)} %param.4) | copy-start | bytes 1474564
  77.3 122.9 %all-gather.5.cloned.1.call-start = ((), (), s32[]{:S(2)}) async-start(), calls=%async_computation.3 | async-start | bytes 2228224 | tf_op jit(solution)/shard_map/all_gather | solution.py:32
  159.6 71.5 %reduce-scatter.5.cloned.1.call-start = ((), (), s32[]{:S(2)}) async-start(), calls=%async_computation.4 | async-start | bytes 786432 | tf_op jit(solution)/shard_map/reduce_scatter | solution.py:39
  217.5 4.1 %copy-start = (bf16[128,8192]{1,0:T(8,128)(2,1)S(1)}, bf16[128,8192]{1,0:T(8,128)(2,1)}, u32[]{:S(2)}) copy-start(bf16[128,8192]{1,0:T(8,128)(2,1)} %all-gather.5.cloned.1.call-done) | copy-start | bytes 6291460
Sparse Core Ops, SparseCore 0:
  10.7 44.1 all-gather.2
  77.4 71.2 reduce-scatter.6
  159.7 40.4 all-gather.4
  217.6 13.4 reduce-scatter.4
where the time goes:
time: 249 us; the launch traced here: 248 us
  waiting for transfers between devices  126 us (51%)
  blocking collectives  45.4 us (18%)
  matrix products  34 us (14%)
  local copies, waits for them, and re-layouts  19.2 us (8%)
  between operations  13.8 us (6%)
  other arithmetic  9.09 us (4%)
    all_gather x1, waiting for transfers between devices, per_device(): lax.all_gather(h_factor.astype(jnp.bfloat16), 'cell', axis=0, tiled=True)  46 us
    all_gather x1, waiting for transfers between devices, per_device(): lax.all_gather(h_updated.astype(jnp.bfloat16), 'cell', axis=0, tiled=True)  40.4 us
    unnamed x5, waiting for transfers between devices  36.1 us
    psum x1, blocking collectives, per_device(): w_totals = lax.psum(jnp.sum(w_factor, axis=0), 'cell')  31.7 us
    unnamed x12, local copies, waits for them, and re-layouts  17.4 us
    dot_general x1, matrix products, per_device(): lax.dot_general(quotient_again, h_new_copy, (((1,), (1,)), ((), ())), pre...  17.3 us
    dot_general x1, matrix products, per_device(): lax.dot_general(columns, quotient, (((0,), (0,)), ((), ())), preferred_el...  16.7 us
    all_gather x1, blocking collectives, per_device(): w_updated = lax.all_gather(w_part, 'gene', axis=1, tiled=True)  8.55 us
  transfers between devices with their start and end apart: 4, of which 4 were waited for; matrix products, arithmetic and copies ran while one was open for 3% of the time, Pallas kernels for 0%

commit v1 on v0

--- a/solution.py
+++ b/solution.py
@@ -2,6 +2,24 @@
 import jax.numpy as jnp
 from jax import lax
 from jax.sharding import PartitionSpec as P
+
+
+def collect(shard, axis, dim):
+    ways, here, step = (lax.axis_size(axis), lax.axis_index(axis), shard.shape[dim])
+    dims = [n * ways if d == dim else n for d, n in enumerate(shard.shape)]
+    full = lax.dynamic_update_slice_in_dim(
+        jnp.zeros(dims, shard.dtype), shard, here * step, axis=dim
+    )
+    going_up = going_down = shard
+    for far in range(1, ways // 2 + 1):
+        going_up = lax.ppermute(going_up, axis, [(d, (d + 1) % ways) for d in range(ways)])
+        full = lax.dynamic_update_slice_in_dim(full, going_up, (here - far) % ways * step, axis=dim)
+        if 2 * far < ways:
+            going_down = lax.ppermute(going_down, axis, [(d, (d - 1) % ways) for d in range(ways)])
+            full = lax.dynamic_update_slice_in_dim(
+                full, going_down, (here + far) % ways * step, axis=dim
+            )
+    return full
 
 
 def per_device(counts, w_factor, h_factor):
@@ -13,7 +31,7 @@
     columns = w_copy
     modeled = jnp.dot(
         columns,
-        lax.all_gather(h_factor.astype(jnp.bfloat16), "cell", axis=0, tiled=True),
+        collect(h_factor.astype(jnp.bfloat16), "cell", 0),
         preferred_element_type=jnp.float32,
     )
     quotient = (counts_float / modeled).astype(jnp.bfloat16)

time: 249 us -> 256 us (1.028)
  starting transfers between devices: 0.34 us -> 32.6 us
  waiting for transfers between devices: 126 us -> 108 us
  matrix products: 34 us -> 31.1 us
    all_gather x1 -> x0, waiting for transfers between devices: 46 us -> none  [per_device(): lax.all_gather(h_factor.astype(jnp.bfloat16), 'cell', axis=0, tiled=True)]
    ppermute x0 -> x15, starting transfers between devices: none -> 32.3 us  [the longest x7 31.8 us: collect(): lax.ppermute(going_down, axis, [(d, (d - 1) % ways) for d in range(ways)])]
    ppermute x0 -> x15, waiting for transfers between devices: none -> 25.7 us  [the longest x8 25.6 us: collect(): lax.ppermute(going_up, axis, [(d, (d + 1) % ways) for d in range(ways)])]
    dot_general x1, matrix products: 16.7 us -> 13.8 us  [per_device(): lax.dot_general(columns, quotient, (((0,), (0,)), ((), ())), preferred_el...]
    unnamed x5 -> x4, waiting for transfers between devices: 36.1 us -> 38.1 us
  transfers between devices with their start and end apart: 4 -> 18, of which waited for: 4 -> 11; matrix products, arithmetic and copies ran while one was open for 3% -> 3% of each run, Pallas kernels for 0% -> 0%
where the time goes in v1:
time: 256 us
  waiting for transfers between devices  108 us (42%)
  blocking collectives  43.4 us (17%)
  starting transfers between devices  32.6 us (13%)
  matrix products  31.1 us (12%)
  local copies, waits for them, and re-layouts  19.3 us (8%)
  between operations  13.9 us (5%)
  other arithmetic  7.52 us (3%)
    all_gather x1, waiting for transfers between devices, per_device(): lax.all_gather(h_updated.astype(jnp.bfloat16), 'cell', axis=0, tiled=True)  40.5 us
    unnamed x4, waiting for transfers between devices  38.1 us
    ppermute x7, starting transfers between devices, collect(): lax.ppermute(going_down, axis, [(d, (d - 1) % ways) for d in range(ways)])  31.8 us
    psum x1, blocking collectives, per_device(): w_totals = lax.psum(jnp.sum(w_factor, axis=0), 'cell')  29.7 us
    ppermute x8, waiting for transfers between devices, collect(): lax.ppermute(going_up, axis, [(d, (d + 1) % ways) for d in range(ways)])  25.6 us
    dot_general x1, matrix products, per_device(): lax.dot_general(quotient_again, h_new_copy, (((1,), (1,)), ((), ())), pre...  17.3 us
    unnamed x12, local copies, waits for them, and re-layouts  17.2 us
    dot_general x1, matrix products, per_device(): lax.dot_general(columns, quotient, (((0,), (0,)), ((), ())), preferred_el...  13.8 us
  transfers between devices with their start and end apart: 18, of which 11 were waited for; matrix products, arithmetic and copies ran while one was open for 3% of the time, Pallas kernels for 0%

profile of v1, /device:TPU:0, one launch (start us, length us, event | category | flops | bytes accessed | tf_op | source)
XLA Modules:
  0.0 256.1 jit_solution(2317339135928164540)
XLA Ops:
  7.4 0.7 copy-done.2
  8.7 5.0 %collective-permute-start.1 = (bf16[8,8192]{1,0:T(8,128)(2,1)S(1)}, bf16[8,8192]{1,0:T(8,128)(2,1)S(1)}, u32[]{:S(2)}, u32[]{:S(2)}) collective-permute-start(bf16[8,8192]{1,0:T(8,128)(2,1)S(1)} %get-tuple-element.9), channel_id=1, source_target_pairs={{0,30},{2,0},{4,2},{6,4},{8,6},{10,8},{12,10},{14,12},{16,14},{18,... | collective-permute-start | bytes 393224 | tf_op jit(solution)/shard_map/ppermute | solution.py:18
  13.7 2.7 %collective-permute-done = bf16[8,8192]{1,0:T(8,128)(2,1)S(1)} collective-permute-done((bf16[8,8192]{1,0:T(8,128)(2,1)S(1)}, bf16[8,8192]{1,0:T(8,128)(2,1)S(1)}, u32[]{:S(2)}, u32[]{:S(2)}) %collective-permute-start) | collective-permute-done | bytes 131104 | tf_op jit(solution)/shard_map/ppermute | solution.py:15
  16.4 4.4 %collective-permute-start.3 = (bf16[8,8192]{1,0:T(8,128)(2,1)S(1)}, bf16[8,8192]{1,0:T(8,128)(2,1)S(1)}, u32[]{:S(2)}, u32[]{:S(2)}) collective-permute-start(bf16[8,8192]{1,0:T(8,128)(2,1)S(1)} %collective-permute-done.1), channel_id=1, source_target_pairs={{0,30},{2,0},{4,2},{6,4},{8,6},{10,8},{12,10},{14,12},{16,14},{18,... | collective-permute-start | bytes 393224 | tf_op jit(solution)/shard_map/ppermute | solution.py:18
  20.9 2.6 %collective-permute-done.2 = bf16[8,8192]{1,0:T(8,128)(2,1)S(1)} collective-permute-done((bf16[8,8192]{1,0:T(8,128)(2,1)S(1)}, bf16[8,8192]{1,0:T(8,128)(2,1)S(1)}, u32[]{:S(2)}, u32[]{:S(2)}) %collective-permute-start.2) | collective-permute-done | bytes 131104 | tf_op jit(solution)/shard_map/ppermute | solution.py:15
  23.5 4.5 %collective-permute-start.5 = (bf16[8,8192]{1,0:T(8,128)(2,1)S(1)}, bf16[8,8192]{1,0:T(8,128)(2,1)S(1)}, u32[]{:S(2)}, u32[]{:S(2)}) collective-permute-start(bf16[8,8192]{1,0:T(8,128)(2,1)S(1)} %collective-permute-done.3), channel_id=1, source_target_pairs={{0,30},{2,0},{4,2},{6,4},{8,6},{10,8},{12,10},{14,12},{16,14},{18,... | collective-permute-start | bytes 393224 | tf_op jit(solution)/shard_map/ppermute | solution.py:18
  28.1 2.6 %collective-permute-done.4 = bf16[8,8192]{1,0:T(8,128)(2,1)S(1)} collective-permute-done((bf16[8,8192]{1,0:T(8,128)(2,1)S(1)}, bf16[8,8192]{1,0:T(8,128)(2,1)S(1)}, u32[]{:S(2)}, u32[]{:S(2)}) %collective-permute-start.4) | collective-permute-done | bytes 131104 | tf_op jit(solution)/shard_map/ppermute | solution.py:15
  30.7 4.4 %collective-permute-start.7 = (bf16[8,8192]{1,0:T(8,128)(2,1)S(1)}, bf16[8,8192]{1,0:T(8,128)(2,1)S(1)}, u32[]{:S(2)}, u32[]{:S(2)}) collective-permute-start(bf16[8,8192]{1,0:T(8,128)(2,1)S(1)} %collective-permute-done.5), channel_id=1, source_target_pairs={{0,30},{2,0},{4,2},{6,4},{8,6},{10,8},{12,10},{14,12},{16,14},{18,... | collective-permute-start | bytes 393224 | tf_op jit(solution)/shard_map/ppermute | solution.py:18
  35.2 2.7 %collective-permute-done.6 = bf16[8,8192]{1,0:T(8,128)(2,1)S(1)} collective-permute-done((bf16[8,8192]{1,0:T(8,128)(2,1)S(1)}, bf16[8,8192]{1,0:T(8,128)(2,1)S(1)}, u32[]{:S(2)}, u32[]{:S(2)}) %collective-permute-start.6) | collective-permute-done | bytes 131104 | tf_op jit(solution)/shard_map/ppermute | solution.py:15
  37.9 4.4 %collective-permute-start.9 = (bf16[8,8192]{1,0:T(8,128)(2,1)S(1)}, bf16[8,8192]{1,0:T(8,128)(2,1)S(1)}, u32[]{:S(2)}, u32[]{:S(2)}) collective-permute-start(bf16[8,8192]{1,0:T(8,128)(2,1)S(1)} %collective-permute-done.7), channel_id=1, source_target_pairs={{0,30},{2,0},{4,2},{6,4},{8,6},{10,8},{12,10},{14,12},{16,14},{18,... | collective-permute-start | bytes 393224 | tf_op jit(solution)/shard_map/ppermute | solution.py:18
  42.4 2.7 %collective-permute-done.8 = bf16[8,8192]{1,0:T(8,128)(2,1)S(1)} collective-permute-done((bf16[8,8192]{1,0:T(8,128)(2,1)S(1)}, bf16[8,8192]{1,0:T(8,128)(2,1)S(1)}, u32[]{:S(2)}, u32[]{:S(2)}) %collective-permute-start.8) | collective-permute-done | bytes 131104 | tf_op jit(solution)/shard_map/ppermute | solution.py:15
  45.1 4.4 %collective-permute-start.11 = (bf16[8,8192]{1,0:T(8,128)(2,1)S(1)}, bf16[8,8192]{1,0:T(8,128)(2,1)S(1)}, u32[]{:S(2)}, u32[]{:S(2)}) collective-permute-start(bf16[8,8192]{1,0:T(8,128)(2,1)S(1)} %collective-permute-done.9), channel_id=1, source_target_pairs={{0,30},{2,0},{4,2},{6,4},{8,6},{10,8},{12,10},{14,12},{16,14},{18,... | collective-permute-start | bytes 393224 | tf_op jit(solution)/shard_map/ppermute | solution.py:18
  49.5 2.7 %collective-permute-done.10 = bf16[8,8192]{1,0:T(8,128)(2,1)S(1)} collective-permute-done((bf16[8,8192]{1,0:T(8,128)(2,1)S(1)}, bf16[8,8192]{1,0:T(8,128)(2,1)S(1)}, u32[]{:S(2)}, u32[]{:S(2)}) %collective-permute-start.10) | collective-permute-done | bytes 131104 | tf_op jit(solution)/shard_map/ppermute | solution.py:15
  52.3 4.4 %collective-permute-start.13 = (bf16[8,8192]{1,0:T(8,128)(2,1)S(1)}, bf16[8,8192]{1,0:T(8,128)(2,1)S(1)}, u32[]{:S(2)}, u32[]{:S(2)}) collective-permute-start(bf16[8,8192]{1,0:T(8,128)(2,1)S(1)} %collective-permute-done.11), channel_id=1, source_target_pairs={{0,30},{2,0},{4,2},{6,4},{8,6},{10,8},{12,10},{14,12},{16,14},{18,... | collective-permute-start | bytes 393224 | tf_op jit(solution)/shard_map/ppermute | solution.py:18
  56.7 2.6 %collective-permute-done.12 = bf16[8,8192]{1,0:T(8,128)(2,1)S(1)} collective-permute-done((bf16[8,8192]{1,0:T(8,128)(2,1)S(1)}, bf16[8,8192]{1,0:T(8,128)(2,1)S(1)}, u32[]{:S(2)}, u32[]{:S(2)}) %collective-permute-start.12) | collective-permute-done | bytes 131104 | tf_op jit(solution)/shard_map/ppermute | solution.py:15
  59.4 7.0 %collective-permute-done.14 = bf16[8,8192]{1,0:T(8,128)(2,1)S(1)} collective-permute-done((bf16[8,8192]{1,0:T(8,128)(2,1)S(1)}, bf16[8,8192]{1,0:T(8,128)(2,1)S(1)}, u32[]{:S(2)}, u32[]{:S(2)}) %collective-permute-start.14) | collective-permute-done | bytes 131104 | tf_op jit(solution)/shard_map/ppermute | solution.py:15
  66.5 13.8 %convolution_bitcast_fusion = f32[128,8192]{0,1:T(8,128)} fusion(bf16[960,8192]{1,0:T(8,128)(2,1)} %param.3, bf16[128,8192]{1,0:T(8,128)(2,1)S(1)} %constant_dynamic-update-slice_fusion, f32[960,128]{1,0:T(8,128)S(1)} %copy-done.1), kind=kOutput, calls=%fused_computation.4 | convolution fusion | flops 4050370560 | bytes 22511616 | tf_op jit(solution)/shard_map/dot_general | solution.py:40
  80.3 5.6 %copy.14 = f32[128,8192]{1,0:T(8,128)} copy(f32[128,8192]{0,1:T(8,128)} %convolution_bitcast_fusion) | data formatting | bytes 8388608
  86.0 2.6 %copy.10 = f32[8,8192]{0,1:T(8,128)} copy(f32[8,8192]{1,0:T(8,128)S(1)} %copy-done.2) | data formatting | bytes 524288 | tf_op args[2]
  88.7 29.7 %psum.14 = f32[128]{0:T(128)S(1)} all-reduce(f32[128]{0:T(128)S(1)} %reduce_sum.18), channel_id=1, replica_groups=mesh['cell'=16,'gene'=2] {'cell'}, use_global_device_ids=true, to_apply=%region_2.3 | all-reduce | flops 128 | bytes 1024 | tf_op jit(solution)/shard_map/psum | solution.py:47
  118.5 38.0 %reduce-scatter.7.cloned.1.call-done = f32[8,8192]{1,0:T(8,128)} async-done(((f32[128,8192]{1,0:T(8,128)}), f32[8,8192]{1,0:T(8,128)}) %reduce-scatter.7.cloned.1.call-update) | async-done | bytes 262160
  156.5 3.5 %copy.15 = f32[8,8192]{0,1:T(8,128)} copy(f32[8,8192]{1,0:T(8,128)} %reduce-scatter.7.cloned.1.call-done) | data formatting | bytes 524288
  160.0 6.0 %fusion.7 = (bf16[8,8192]{0,1:T(8,128)(2,1)S(1)}, f32[8,8192]{0,1:T(8,128)}) fusion(f32[8]{0:T(128)S(1)} %dynamic_slice.10, f32[8,8192]{0,1:T(8,128)} %copy.10, f32[8,8192]{0,1:T(8,128)} %copy.15), kind=kLoop, calls=%fused_computation.28 | loop fusion | flops 196608 | bytes 917536 | tf_op jit(solution)/shard_map/convert_element_type | solution.py:50
  166.0 1.4 copy.11
  167.6 40.5 %all-gather.2.cloned.1.call-done = bf16[128,8192]{1,0:T(8,128)(2,1)} async-done(((bf16[8,8192]{1,0:T(8,128)(2,1)}), bf16[128,8192]{1,0:T(8,128)(2,1)}) %all-gather.2.cloned.1.call-update) | async-done | bytes 2097168 | tf_op jit(solution)/shard_map/all_gather | solution.py:50
  208.1 17.3 %fusion.2 = f32[960,128]{0,1:T(8,128)} fusion(bf16[128,8192]{1,0:T(8,128)(2,1)} %all-gather.2.cloned.1.call-done, bf16[960,8192]{1,0:T(8,128)(2,1)} %param.3, f32[960,128]{1,0:T(8,128)S(1)} %copy-done.1), kind=kOutput, calls=%fused_computation.5 | convolution fusion | flops 4050247680 | bytes 18808832 | tf_op jit(solution)/shard_map/dot_general | solution.py:53
  225.8 3.6 %copy.13 = f32[8,8192]{1,0:T(8,128)} copy(f32[8,8192]{0,1:T(8,128)} %get-tuple-element.7) | data formatting | bytes 524288
  229.8 5.1 %psum.15 = f32[128]{0:T(128)S(1)} all-reduce(f32[128]{0:T(128)S(1)} %convert_reduce_fusion), channel_id=1, replica_groups=mesh['cell'=16,'gene'=2] {'gene'}, use_global_device_ids=true, to_apply=%region_5.6 | all-reduce | flops 128 | bytes 1024 | tf_op jit(solution)/shard_map/psum | solution.py:58
  235.0 4.0 %reduce-scatter.5.cloned.1.call-done = f32[960,64]{0,1:T(8,128)} async-done(((f32[960,128]{0,1:T(8,128)}), f32[960,64]{0,1:T(8,128)}) %reduce-scatter.5.cloned.1.call-update) | async-done | bytes 245776 | tf_op jit(solution)/shard_map/reduce_scatter | solution.py:57
  239.0 1.0 multiply_divide_fusion.1
  240.1 8.5 %all_gather.7 = f32[960,128]{0,1:T(8,128)S(1)} all-gather(f32[960,64]{0,1:T(8,128)S(1)} %multiply_divide_fusion.1), channel_id=1, replica_groups=mesh['cell'=16,'gene'=2] {'gene'}, dimensions={1}, use_global_device_ids=true | all-gather | bytes 737280 | tf_op jit(solution)/shard_map/all_gather | solution.py:64
  248.6 1.0 copy.12
  (49 shorter events, 2.4 us)
Async XLA Ops:
  7.2 1.0 copy-start.2
  7.2 149.3 %reduce-scatter.7.cloned.1.call-start = ((), (), s32[]{:S(2)}) async-start(), calls=%async_computation.4 | async-start | bytes 4456448
  8.1 8.3 %collective-permute-start = (bf16[8,8192]{1,0:T(8,128)(2,1)S(1)}, bf16[8,8192]{1,0:T(8,128)(2,1)S(1)}, u32[]{:S(2)}, u32[]{:S(2)}) collective-permute-start(bf16[8,8192]{1,0:T(8,128)(2,1)S(1)} %get-tuple-element.9), channel_id=1, source_target_pairs={{0,2},{2,4},{4,6},{6,8},{8,10},{10,12},{12,14},{14,16},{16,18},{18... | collective-permute-start | bytes 393224 | tf_op jit(solution)/shard_map/ppermute | solution.py:15
  8.7 7.7 %collective-permute-start.1 = (bf16[8,8192]{1,0:T(8,128)(2,1)S(1)}, bf16[8,8192]{1,0:T(8,128)(2,1)S(1)}, u32[]{:S(2)}, u32[]{:S(2)}) collective-permute-start(bf16[8,8192]{1,0:T(8,128)(2,1)S(1)} %get-tuple-element.9), channel_id=1, source_target_pairs={{0,30},{2,0},{4,2},{6,4},{8,6},{10,8},{12,10},{14,12},{16,14},{18,... | collective-permute-start | bytes 393224 | tf_op jit(solution)/shard_map/ppermute | solution.py:18
  13.7 52.7 %copy-start.1 = (f32[960,128]{1,0:T(8,128)S(1)}, f32[960,128]{1,0:T(8,128)}, u32[]{:S(2)}) copy-start(f32[960,128]{1,0:T(8,128)} %param.4) | copy-start | bytes 1474564
  16.4 7.1 %collective-permute-start.2 = (bf16[8,8192]{1,0:T(8,128)(2,1)S(1)}, bf16[8,8192]{1,0:T(8,128)(2,1)S(1)}, u32[]{:S(2)}, u32[]{:S(2)}) collective-permute-start(bf16[8,8192]{1,0:T(8,128)(2,1)S(1)} %collective-permute-done), channel_id=1, source_target_pairs={{0,2},{2,4},{4,6},{6,8},{8,10},{10,12},{12,14},{14,16},{16,18},{18... | collective-permute-start | bytes 393224 | tf_op jit(solution)/shard_map/ppermute | solution.py:15
  16.4 7.1 %collective-permute-start.3 = (bf16[8,8192]{1,0:T(8,128)(2,1)S(1)}, bf16[8,8192]{1,0:T(8,128)(2,1)S(1)}, u32[]{:S(2)}, u32[]{:S(2)}) collective-permute-start(bf16[8,8192]{1,0:T(8,128)(2,1)S(1)} %collective-permute-done.1), channel_id=1, source_target_pairs={{0,30},{2,0},{4,2},{6,4},{8,6},{10,8},{12,10},{14,12},{16,14},{18,... | collective-permute-start | bytes 393224 | tf_op jit(solution)/shard_map/ppermute | solution.py:18
  23.5 7.2 %collective-permute-start.4 = (bf16[8,8192]{1,0:T(8,128)(2,1)S(1)}, bf16[8,8192]{1,0:T(8,128)(2,1)S(1)}, u32[]{:S(2)}, u32[]{:S(2)}) collective-permute-start(bf16[8,8192]{1,0:T(8,128)(2,1)S(1)} %collective-permute-done.2), channel_id=1, source_target_pairs={{0,2},{2,4},{4,6},{6,8},{8,10},{10,12},{12,14},{14,16},{16,18},{18... | collective-permute-start | bytes 393224 | tf_op jit(solution)/shard_map/ppermute | solution.py:15
  23.5 7.2 %collective-permute-start.5 = (bf16[8,8192]{1,0:T(8,128)(2,1)S(1)}, bf16[8,8192]{1,0:T(8,128)(2,1)S(1)}, u32[]{:S(2)}, u32[]{:S(2)}) collective-permute-start(bf16[8,8192]{1,0:T(8,128)(2,1)S(1)} %collective-permute-done.3), channel_id=1, source_target_pairs={{0,30},{2,0},{4,2},{6,4},{8,6},{10,8},{12,10},{14,12},{16,14},{18,... | collective-permute-start | bytes 393224 | tf_op jit(solution)/shard_map/ppermute | solution.py:18
  30.7 7.2 %collective-permute-start.6 = (bf16[8,8192]{1,0:T(8,128)(2,1)S(1)}, bf16[8,8192]{1,0:T(8,128)(2,1)S(1)}, u32[]{:S(2)}, u32[]{:S(2)}) collective-permute-start(bf16[8,8192]{1,0:T(8,128)(2,1)S(1)} %collective-permute-done.4), channel_id=1, source_target_pairs={{0,2},{2,4},{4,6},{6,8},{8,10},{10,12},{12,14},{14,16},{16,18},{18... | collective-permute-start | bytes 393224 | tf_op jit(solution)/shard_map/ppermute | solution.py:15
  30.7 7.2 %collective-permute-start.7 = (bf16[8,8192]{1,0:T(8,128)(2,1)S(1)}, bf16[8,8192]{1,0:T(8,128)(2,1)S(1)}, u32[]{:S(2)}, u32[]{:S(2)}) collective-permute-start(bf16[8,8192]{1,0:T(8,128)(2,1)S(1)} %collective-permute-done.5), channel_id=1, source_target_pairs={{0,30},{2,0},{4,2},{6,4},{8,6},{10,8},{12,10},{14,12},{16,14},{18,... | collective-permute-start | bytes 393224 | tf_op jit(solution)/shard_map/ppermute | solution.py:18
  37.9 7.2 %collective-permute-start.8 = (bf16[8,8192]{1,0:T(8,128)(2,1)S(1)}, bf16[8,8192]{1,0:T(8,128)(2,1)S(1)}, u32[]{:S(2)}, u32[]{:S(2)}) collective-permute-start(bf16[8,8192]{1,0:T(8,128)(2,1)S(1)} %collective-permute-done.6), channel_id=1, source_target_pairs={{0,2},{2,4},{4,6},{6,8},{8,10},{10,12},{12,14},{14,16},{16,18},{18... | collective-permute-start | bytes 393224 | tf_op jit(solution)/shard_map/ppermute | solution.py:15
  37.9 7.2 %collective-permute-start.9 = (bf16[8,8192]{1,0:T(8,128)(2,1)S(1)}, bf16[8,8192]{1,0:T(8,128)(2,1)S(1)}, u32[]{:S(2)}, u32[]{:S(2)}) collective-permute-start(bf16[8,8192]{1,0:T(8,128)(2,1)S(1)} %collective-permute-done.7), channel_id=1, source_target_pairs={{0,30},{2,0},{4,2},{6,4},{8,6},{10,8},{12,10},{14,12},{16,14},{18,... | collective-permute-start | bytes 393224 | tf_op jit(solution)/shard_map/ppermute | solution.py:18
  45.1 7.2 %collective-permute-start.10 = (bf16[8,8192]{1,0:T(8,128)(2,1)S(1)}, bf16[8,8192]{1,0:T(8,128)(2,1)S(1)}, u32[]{:S(2)}, u32[]{:S(2)}) collective-permute-start(bf16[8,8192]{1,0:T(8,128)(2,1)S(1)} %collective-permute-done.8), channel_id=1, source_target_pairs={{0,2},{2,4},{4,6},{6,8},{8,10},{10,12},{12,14},{14,16},{16,18},{18... | collective-permute-start | bytes 393224 | tf_op jit(solution)/shard_map/ppermute | solution.py:15
  45.1 7.2 %collective-permute-start.11 = (bf16[8,8192]{1,0:T(8,128)(2,1)S(1)}, bf16[8,8192]{1,0:T(8,128)(2,1)S(1)}, u32[]{:S(2)}, u32[]{:S(2)}) collective-permute-start(bf16[8,8192]{1,0:T(8,128)(2,1)S(1)} %collective-permute-done.9), channel_id=1, source_target_pairs={{0,30},{2,0},{4,2},{6,4},{8,6},{10,8},{12,10},{14,12},{16,14},{18,... | collective-permute-start | bytes 393224 | tf_op jit(solution)/shard_map/ppermute | solution.py:18
  52.2 7.1 %collective-permute-start.12 = (bf16[8,8192]{1,0:T(8,128)(2,1)S(1)}, bf16[8,8192]{1,0:T(8,128)(2,1)S(1)}, u32[]{:S(2)}, u32[]{:S(2)}) collective-permute-start(bf16[8,8192]{1,0:T(8,128)(2,1)S(1)} %collective-permute-done.10), channel_id=1, source_target_pairs={{0,2},{2,4},{4,6},{6,8},{8,10},{10,12},{12,14},{14,16},{16,18},{18... | collective-permute-start | bytes 393224 | tf_op jit(solution)/shard_map/ppermute | solution.py:15
  52.3 7.1 %collective-permute-start.13 = (bf16[8,8192]{1,0:T(8,128)(2,1)S(1)}, bf16[8,8192]{1,0:T(8,128)(2,1)S(1)}, u32[]{:S(2)}, u32[]{:S(2)}) collective-permute-start(bf16[8,8192]{1,0:T(8,128)(2,1)S(1)} %collective-permute-done.11), channel_id=1, source_target_pairs={{0,30},{2,0},{4,2},{6,4},{8,6},{10,8},{12,10},{14,12},{16,14},{18,... | collective-permute-start | bytes 393224 | tf_op jit(solution)/shard_map/ppermute | solution.py:18
  59.3 7.1 %collective-permute-start.14 = (bf16[8,8192]{1,0:T(8,128)(2,1)S(1)}, bf16[8,8192]{1,0:T(8,128)(2,1)S(1)}, u32[]{:S(2)}, u32[]{:S(2)}) collective-permute-start(bf16[8,8192]{1,0:T(8,128)(2,1)S(1)} %collective-permute-done.12), channel_id=1, source_target_pairs={{0,2},{2,4},{4,6},{6,8},{8,10},{10,12},{12,14},{14,16},{16,18},{18... | collective-permute-start | bytes 393224 | tf_op jit(solution)/shard_map/ppermute | solution.py:15
  85.9 122.2 %all-gather.2.cloned.1.call-start = ((), (), s32[]{:S(2)}) async-start(), calls=%async_computation.2 | async-start | bytes 2228224 | tf_op jit(solution)/shard_map/all_gather | solution.py:50
  167.4 71.6 %reduce-scatter.5.cloned.1.call-start = ((), (), s32[]{:S(2)}) async-start(), calls=%async_computation.3 | async-start | bytes 786432 | tf_op jit(solution)/shard_map/reduce_scatter | solution.py:57
  225.8 3.6 %copy-start = (bf16[128,8192]{1,0:T(8,128)(2,1)S(1)}, bf16[128,8192]{1,0:T(8,128)(2,1)}, u32[]{:S(2)}) copy-start(bf16[128,8192]{1,0:T(8,128)(2,1)} %all-gather.2.cloned.1.call-done) | copy-start | bytes 6291460
Sparse Core Ops, SparseCore 0:
  86.0 70.4 reduce-scatter.6
  167.5 40.5 all-gather.1
  225.6 13.4 reduce-scatter.4
